TPU v7x, 128 devices: a whole 4x4x4 slice. The times are simulated.
128 devices in a mesh: tm: 16 (over y, z), env: 8 (over x, core).
Axes of the slice: x: 4, y: 4, z: 4, core: 2. Of those that a mesh axis runs over, the one named last changes fastest.
Arguments:
- rewards: float32 [32768, 4096], P('tm', 'env'), may hold values from -0.16 to 0.16
- values: float32 [32768, 4096], P('tm', 'env'), may hold values from -6 to 6
- last_value: float32 [4096], P('env'), may hold values from -6 to 6
- done_steps: int32 [4096, 4], P('env'), may hold values from 0 to 32767
- horizon_offset: int32 [4096], P('env'), may hold values from 0 to 16383
- discount_rate: float32 [4096], P('env'), may hold values from 1.5258789e-06 to 0.03
- trace_rate: float32 [4096], P('env'), may hold values from 1.5258789e-06 to 0.03
Outputs:
- norm_advantages: float32 [4096, 32768], P(('env', 'tm'))
- norm_returns: float32 [4096, 32768], P(('env', 'tm'))
Inputs may be any that keep to these rules, and one draw needn't show every extreme that they name: `done_steps`: a repeated step in one environment's list is one termination.
All inputs are finite; a program needn't handle non-finite values.
Results may differ from a plain program's by a relative error of at most 0.0008.
Values sent between devices are 32-bit elements; how exact they have to be, the bound alone decides.
No kernel may reach another device: no remote copies, remote signals or barrier semaphores. Data moves between devices by JAX's collectives and lax.ppermute only.
A program may use at most 128 MiB of HBM per device.

v0:
```python
import jax
import jax.numpy as jnp
from jax import lax
from jax.sharding import Mesh
from jax.sharding import PartitionSpec as P

TM = ("tm_0", "tm_1")
ENV = ("env_0", "env_1")
TM_ENV = ("tm_0", "tm_1", "env_0", "env_1")
ENV_TM = ("env_0", "env_1", "tm_0", "tm_1")


def by_axis(value, axes):
    for axis in axes:
        value = lax.psum(value, axis)
    return value


def from_behind(block, axis, distance):
    devices = range(lax.axis_size(axis))
    route = [(i - distance, i) for i in devices if i - distance in devices]
    return lax.ppermute(block, axis, route)


def copy_for_each(value, axis):
    size = lax.axis_size(axis)
    return lax.all_to_all(
        jnp.broadcast_to(value[None], (size, *value.shape)), axis, 0, 0, tiled=True
    )


def all_in_one(value, axis):
    leaves = jax.tree.leaves(value)
    order = sorted(range(len(leaves)), key=lambda k: -leaves[k].size)
    width = (1, *leaves[order[0]].shape)[-1]
    lines = [
        jnp.pad(leaves[k].reshape(-1), (0, -leaves[k].size % width)).reshape(-1, width)
        for k in order
    ]
    both, at, found = (copy_for_each(jnp.concatenate(lines), axis), 0, {})
    for k, line in zip(order, lines):
        piece = both[:, at : at + len(line)].reshape(len(both), -1)
        found[k] = piece[:, : leaves[k].size].reshape(-1, *leaves[k].shape)
        at += len(line)
    numbers = iter(range(len(leaves)))
    return jax.tree.map(lambda _: found[next(numbers)], value)


def combined_pairwise(pieces, combine):
    while len(jax.tree.leaves(pieces)[0]) > 1:
        pieces = jax.vmap(combine)(
            *(jax.tree.map(lambda part: part[side::2], pieces) for side in (0, 1))
        )
    return jax.tree.map(lambda part: part[0], pieces)


def prefix(value, axis, combine, identity):
    size, here = (lax.axis_size(axis), lax.axis_index(axis))
    passed = jnp.arange(size) > here

    def kept(part, zero, own):
        part = jnp.where(
            passed.reshape(-1, *(1 for _ in own.shape)), part, jnp.asarray(zero, own.dtype)
        )
        return part[::-1]

    pieces = all_in_one(value, axis)
    return combined_pairwise(jax.tree.map(kept, pieces, identity, value), combine)


def episode_masks(moment_index, ends, offsets, horizon):
    finished = jnp.zeros_like(moment_index + offsets, dtype=bool)
    for column in ends:
        finished = finished | (moment_index == column)
    truncated = (moment_index + offsets) % horizon == horizon - 1
    living = 1.0 - finished.astype(jnp.float32)
    carried = living * (1.0 - truncated.astype(jnp.float32))
    return (living, carried)


def shift_later(field, distance, axis, filler):
    length = field.shape[axis]
    kept = lax.slice_in_dim(field, distance, length, 1, axis)
    shape = list(field.shape)
    shape[axis] = distance
    pad_block = jnp.full(tuple(shape), filler, field.dtype)
    return jnp.concatenate([kept, pad_block], axis=axis)


def suffix_scan(td_error, decay, axis):
    length = td_error.shape[axis]
    partial_value = td_error
    decayed = decay
    distance = 1
    while distance < length:
        later_partial = shift_later(partial_value, distance, axis, 0.0)
        later_decayed = shift_later(decayed, distance, axis, 1.0)
        partial_value = partial_value + decayed * later_partial
        decayed = decayed * later_decayed
        distance = distance * 2
    return (partial_value, decayed)


def compose_blocks(earlier, later):
    return (later[0] + later[1] * earlier[0], later[1] * earlier[1])


def statistics(advantages, returns):
    devices = lax.axis_size(TM) * lax.axis_size(ENV)
    samples = float(advantages.size * devices)
    sum_adv, sum_ret = (by_axis(jnp.sum(advantages), TM_ENV), by_axis(jnp.sum(returns), TM_ENV))
    mean_adv = sum_adv / samples
    mean_ret = sum_ret / samples
    dev_adv = advantages - mean_adv
    dev_ret = returns - mean_ret
    sq_adv, sq_ret = (
        by_axis(jnp.sum(dev_adv * dev_adv), TM_ENV),
        by_axis(jnp.sum(dev_ret * dev_ret), TM_ENV),
    )
    var_adv = sq_adv / samples
    var_ret = sq_ret / samples
    norm_adv = (advantages - mean_adv) / jnp.sqrt(var_adv + 1e-05)
    norm_ret = (returns - mean_ret) / jnp.sqrt(var_ret + 1e-05)
    return (norm_adv, norm_ret)


def shards(rewards, values, last_value, done_steps, horizon_offset, discount_rate, trace_rate):
    steps_dev, envs_dev = rewards.shape
    time_blocks = lax.axis_size(TM)
    position = lax.axis_index(TM)
    horizon = steps_dev * time_blocks // 2
    discount = jnp.exp(-discount_rate)
    retention = discount * jnp.exp(-trace_rate)
    moment_index = position * steps_dev + jnp.arange(steps_dev, dtype=jnp.int32)[:, None]
    ends = [done_steps[:, column][None, :] for column in range(done_steps.shape[1])]
    living, carried = episode_masks(moment_index, ends, horizon_offset[None, :], horizon)
    first_next = from_behind(values[0:1], TM, -1)
    boundary = jnp.where(position == time_blocks - 1, last_value[None, :], first_next)
    next_value = jnp.concatenate([values[1:], boundary], axis=0)
    td_error = rewards + discount[None, :] * living * next_value - values
    decay = retention[None, :] * carried
    partial_value, decayed = suffix_scan(td_error, decay, 0)
    identity = (jnp.zeros_like(partial_value[0]), jnp.ones_like(decayed[0]))
    incoming = prefix((partial_value[0], decayed[0]), TM, compose_blocks, identity)[0]
    advantages = partial_value + decayed * incoming[None, :]
    returns = advantages + values
    norm_adv, norm_ret = statistics(advantages, returns)
    return (
        lax.all_to_all(norm_adv.T, TM, split_axis=0, concat_axis=1, tiled=True),
        lax.all_to_all(norm_ret.T, TM, split_axis=0, concat_axis=1, tiled=True),
    )


def solution(mesh):
    split = Mesh(mesh.devices.reshape(4, 4, 4, 2), ("tm_0", "tm_1", "env_0", "env_1"))
    placed = (P(TM, ENV), P(TM, ENV), P(ENV), P(ENV, None), P(ENV), P(ENV), P(ENV))
    return jax.shard_map(
        shards,
        mesh=split,
        in_specs=placed,
        out_specs=(P(ENV_TM, None), P(ENV_TM, None)),
        check_vma=False,
    )
```

profile of v0, /device:TPU:114, one launch (start us, length us, event | category | flops | bytes accessed | tf_op | source)
XLA Modules:
  0.0 445.4 jit_solution(117539721496437873)
XLA Ops:
  5.2 5.3 %copy.25 = f32[2048,512]{0,1:T(8,128)} copy(f32[2048,512]{1,0:T(8,128)} %param.8) | data formatting | bytes 8388608 | tf_op args[1]
  10.6 5.3 %slice.207 = f32[2047,512]{0,1:T(8,128)} slice(f32[2048,512]{0,1:T(8,128)} %copy.25), slice={[1:2048], [0:512]} | slice | bytes 8384512 | tf_op jit(solution)/shard_map/slice | solution.py:139
  15.9 5.3 %copy.27 = f32[2048,512]{0,1:T(8,128)} copy(f32[2048,512]{1,0:T(8,128)} %param.7) | data formatting | bytes 8388608 | tf_op args[0]
  21.4 6.0 %fusion.3 = f32[2048,512]{0,1:T(8,128)S(1)} fusion(f32[2048,512]{0,1:T(8,128)} %copy.25, f32[2048,512]{0,1:T(8,128)} %copy.27, f32[1,512]{0,1:T(8,128)S(1)} %copy.26, f32[2047,512]{0,1:T(8,128)} %slice.207, f32[512]{0:T(512)S(1)} %get-tuple-element.54, s32[512]{0:T(512)S(1)} %bitcast.34, s32[512]{0:T(512)S(1)} %bitcast.37, s32[512]{0:T(512)S(1)} %bitcast.31, ...), kind=kLoop, calls=%fused_computation.9 | loop fusion | flops 14680064 | bytes 16795648 | tf_op jit(solution)/shard_map/sub | solution.py:140
  28.6 5.3 %multiply_multiply_fusion = (f32[2048,512]{0,1:T(8,128)S(1)}, f32[2048,512]{0,1:T(8,128)S(1)}) fusion(s32[512]{0:T(512)S(1)} %copy-done.18, f32[512]{0:T(512)S(1)} %get-tuple-element.53, s32[2048]{0:T(1024)S(1)} %iota_add_fusion, s32[512]{0:T(512)S(1)} %bitcast.35, s32[512]{0:T(512)S(1)} %bitcast.38, s32[512]{0:T(512)S(1)} %bitcast.32, s32[512]{0:T(512)S(1)} %bitcast.29, ...), kind=kLoop, calls=%fused_computation.35 | loop fusion | flops 29360128 | bytes 16795648 | tf_op jit(solution)/shard_map/mul | solution.py:141
  36.1 5.7 %multiply_add_fusion.10 = (f32[2048,512]{0,1:T(8,128)S(1)}, f32[2048,512]{0,1:T(8,128)S(1)}) fusion(f32[2048,512]{0,1:T(8,128)S(1)} %get-tuple-element.44, f32[2046,512]{0,1:T(8,128)S(1)} %slice.210, f32[2047,512]{0,1:T(8,128)S(1)} %slice.209, s32[512]{0:T(512)S(1)} %copy-done.18, s32[512]{0:T(512)S(1)} %bitcast.36, s32[512]{0:T(512)S(1)} %bitcast.39, ...), kind=kLoop, calls=%fused_computation.32 | loop fusion | flops 30408704 | bytes 20985856 | tf_op jit(solution)/shard_map/add | solution.py:98
  41.8 3.4 slice.212
  48.3 10.2 %multiply_add_fusion.9 = (f32[2048,512]{0,1:T(8,128)}, f32[2048,512]{0,1:T(8,128)}) fusion(f32[2048,512]{0,1:T(8,128)S(1)} %get-tuple-element.39, f32[2044,512]{0,1:T(8,128)} %slice.212, f32[2048,512]{0,1:T(8,128)} %copy-done, f32[2046,512]{0,1:T(8,128)} %slice.211), kind=kLoop, calls=%fused_computation.30 | loop fusion | flops 3145728 | bytes 25153536 | tf_op jit(solution)/shard_map/add | solution.py:98
  58.5 5.5 %slice.214 = f32[2040,512]{0,1:T(8,128)} slice(f32[2048,512]{0,1:T(8,128)} %get-tuple-element.37), slice={[8:2048], [0:512]} | slice | bytes 8355840 | tf_op jit(solution)/shard_map/slice | solution.py:83
  64.0 3.1 slice.213
  67.1 10.2 %multiply_add_fusion.8 = (f32[2048,512]{0,1:T(8,128)}, f32[2048,512]{0,1:T(8,128)}) fusion(f32[2048,512]{0,1:T(8,128)S(1)} %copy-done.1, f32[2040,512]{0,1:T(8,128)} %slice.214, f32[2048,512]{0,1:T(8,128)} %get-tuple-element.38, f32[2044,512]{0,1:T(8,128)} %slice.213), kind=kLoop, calls=%fused_computation.28 | loop fusion | flops 3145728 | bytes 25141248 | tf_op jit(solution)/shard_map/add | solution.py:98
  77.3 5.5 %slice.216 = f32[2032,512]{0,1:T(8,128)} slice(f32[2048,512]{0,1:T(8,128)} %get-tuple-element.35), slice={[16:2048], [0:512]} | slice | bytes 8323072 | tf_op jit(solution)/shard_map/slice | solution.py:83
  82.8 3.1 slice.215
  85.9 10.4 %multiply_add_fusion.7 = (f32[2048,512]{0,1:T(8,128)}, f32[2048,512]{0,1:T(8,128)}) fusion(f32[2048,512]{0,1:T(8,128)S(1)} %copy-done.3, f32[2032,512]{0,1:T(8,128)} %slice.216, f32[2048,512]{0,1:T(8,128)} %get-tuple-element.36, f32[2040,512]{0,1:T(8,128)} %slice.215), kind=kLoop, calls=%fused_computation.26 | loop fusion | flops 3145728 | bytes 25116672 | tf_op jit(solution)/shard_map/add | solution.py:98
  96.3 5.5 %slice.218 = f32[2016,512]{0,1:T(8,128)} slice(f32[2048,512]{0,1:T(8,128)} %get-tuple-element.33), slice={[32:2048], [0:512]} | slice | bytes 8257536 | tf_op jit(solution)/shard_map/slice | solution.py:83
  101.8 3.1 slice.217
  104.9 10.2 %multiply_add_fusion.6 = (f32[2048,512]{0,1:T(8,128)}, f32[2048,512]{0,1:T(8,128)}) fusion(f32[2048,512]{0,1:T(8,128)S(1)} %copy-done.5, f32[2016,512]{0,1:T(8,128)} %slice.218, f32[2048,512]{0,1:T(8,128)} %get-tuple-element.34, f32[2032,512]{0,1:T(8,128)} %slice.217), kind=kLoop, calls=%fused_computation.24 | loop fusion | flops 3145728 | bytes 25067520 | tf_op jit(solution)/shard_map/add | solution.py:98
  115.0 5.5 %slice.220 = f32[1984,512]{0,1:T(8,128)} slice(f32[2048,512]{0,1:T(8,128)} %get-tuple-element.31), slice={[64:2048], [0:512]} | slice | bytes 8126464 | tf_op jit(solution)/shard_map/slice | solution.py:83
  123.7 10.2 %multiply_add_fusion.5 = (f32[2048,512]{0,1:T(8,128)}, f32[2048,512]{0,1:T(8,128)}) fusion(f32[2048,512]{0,1:T(8,128)S(1)} %copy-done.7, f32[1984,512]{0,1:T(8,128)} %slice.220, f32[2048,512]{0,1:T(8,128)} %get-tuple-element.32, f32[2016,512]{0,1:T(8,128)} %slice.219), kind=kLoop, calls=%fused_computation.22 | loop fusion | flops 3145728 | bytes 24969216 | tf_op jit(solution)/shard_map/add | solution.py:98
  133.8 4.4 slice.222
  138.2 3.2 slice.221
  141.4 10.2 %multiply_add_fusion.4 = (f32[2048,512]{0,1:T(8,128)}, f32[2048,512]{0,1:T(8,128)}) fusion(f32[2048,512]{0,1:T(8,128)} %get-tuple-element.29, f32[1920,512]{0,1:T(8,128)} %slice.222, f32[2048,512]{0,1:T(8,128)S(1)} %copy-done.9, f32[1984,512]{0,1:T(8,128)} %slice.221), kind=kLoop, calls=%fused_computation.20 | loop fusion | flops 3145728 | bytes 24772608 | tf_op jit(solution)/shard_map/add | solution.py:98
  151.6 4.2 slice.224
  156.1 8.3 %multiply_add_fusion.3 = (f32[2048,512]{0,1:T(8,128)}, f32[2048,512]{0,1:T(8,128)}) fusion(f32[2048,512]{0,1:T(8,128)} %get-tuple-element.27, f32[1792,512]{0,1:T(8,128)} %slice.224, f32[2048,512]{0,1:T(8,128)S(1)} %copy-done.10, f32[1920,512]{0,1:T(8,128)S(1)} %slice.223), kind=kLoop, calls=%fused_computation.18 | loop fusion | flops 3145728 | bytes 24379392 | tf_op jit(solution)/shard_map/add | solution.py:98
  164.4 4.0 slice.226
  171.9 8.0 %multiply_add_fusion.2 = (f32[2048,512]{0,1:T(8,128)}, f32[2048,512]{0,1:T(8,128)}) fusion(f32[2048,512]{0,1:T(8,128)S(1)} %copy-done.12, f32[1536,512]{0,1:T(8,128)} %slice.226, f32[2048,512]{0,1:T(8,128)S(1)} %copy-done.11, f32[1792,512]{0,1:T(8,128)} %slice.225), kind=kLoop, calls=%fused_computation.16 | loop fusion | flops 3145728 | bytes 23592960 | tf_op jit(solution)/shard_map/add | solution.py:98
  179.9 3.4 slice.228
  186.6 6.7 %multiply_add_fusion.1 = (f32[2048,512]{0,1:T(8,128)S(1)}, f32[2048,512]{0,1:T(8,128)}) fusion(f32[2048,512]{0,1:T(8,128)S(1)} %copy-done.14, f32[1024,512]{0,1:T(8,128)} %slice.228, f32[2048,512]{0,1:T(8,128)S(1)} %copy-done.13, f32[1536,512]{0,1:T(8,128)} %slice.227), kind=kLoop, calls=%fused_computation.14 | loop fusion | flops 3145728 | bytes 22020096 | tf_op jit(solution)/shard_map/add | solution.py:98
  201.9 7.1 %all-to-all-start = ((f32[16,2,512]{2,1,0:T(2,128)}), f32[16,2,512]{2,1,0:T(2,128)S(1)}, u32[]{:S(2)}, u32[]{:S(2)}) async-start(f32[16,2,512]{2,1,0:T(2,128)} %broadcast_in_dim.20), calls=%async_computation | async-start | bytes 131072 | tf_op jit(solution)/shard_map/all_to_all | solution.py:27
  209.0 4.0 all-to-all-done
  213.8 11.1 %fusion.6 = (f32[]{:T(128)}, f32[2048,512]{0,1:T(8,128)}, f32[2048,512]{0,1:T(8,128)}) fusion(f32[2048,512]{0,1:T(8,128)} %copy.25, f32[2048,512]{0,1:T(8,128)} %copy-done.17, f32[2048,512]{0,1:T(8,128)} %copy-done.16, f32[512]{0:T(512)S(1)} %bitcast.40), kind=kLoop, calls=%fused_computation.55 | loop fusion | flops 4194303 | bytes 20973572 | tf_op jit(solution)/shard_map/reduce_sum | solution.py:111
  224.9 3.9 reduce_sum.36
  228.8 9.1 %all-reduce.27 = (f32[]{:T(128)}, f32[]{:T(128)}) all-reduce(f32[]{:T(128)} %reduce_sum.36, f32[]{:T(128)} %get-tuple-element.18), channel_id=1, replica_groups=mesh['tm_0'=4,'tm_1'=4,'env_0'=4,'env_1'=2] {'tm_0'}, use_global_device_ids=true, to_apply=%region_1.2 | all-reduce | flops 2 | bytes 16 | tf_op jit(solution)/shard_map/psum | solution.py:15
  237.9 9.2 %all-reduce.25 = (f32[]{:T(128)}, f32[]{:T(128)}) all-reduce(f32[]{:T(128)} %get-tuple-element.12, f32[]{:T(128)} %get-tuple-element.13), channel_id=1, replica_groups=mesh['tm_0'=4,'tm_1'=4,'env_0'=4,'env_1'=2] {'tm_1'}, use_global_device_ids=true, to_apply=%region_2.3 | all-reduce | flops 2 | bytes 16 | tf_op jit(solution)/shard_map/psum | solution.py:15
  247.1 9.2 %all-reduce.23 = (f32[]{:T(128)}, f32[]{:T(128)}) all-reduce(f32[]{:T(128)} %get-tuple-element.8, f32[]{:T(128)} %get-tuple-element.9), channel_id=1, replica_groups=mesh['tm_0'=4,'tm_1'=4,'env_0'=4,'env_1'=2] {'env_0'}, use_global_device_ids=true, to_apply=%region_3.4 | all-reduce | flops 2 | bytes 16 | tf_op jit(solution)/shard_map/psum | solution.py:15
  256.4 3.3 all-reduce.29
  261.1 5.2 %multiply_reduce_fusion = (f32[]{:T(128)}, f32[]{:T(128)}) fusion(f32[2048,512]{0,1:T(8,128)} %get-tuple-element.19, f32[]{:T(128)S(6)} %div.28, f32[2048,512]{0,1:T(8,128)} %get-tuple-element.20, f32[]{:T(128)S(6)} %div.24), kind=kLoop, calls=%fused_computation.10 | loop fusion | flops 6291454 | bytes 8388624 | tf_op jit(solution)/shard_map/reduce_sum | solution.py:118
  266.2 9.3 %all-reduce.26 = (f32[]{:T(128)}, f32[]{:T(128)}) all-reduce(f32[]{:T(128)} %get-tuple-element.58, f32[]{:T(128)} %get-tuple-element.57), channel_id=1, replica_groups=mesh['tm_0'=4,'tm_1'=4,'env_0'=4,'env_1'=2] {'tm_0'}, use_global_device_ids=true, to_apply=%region_6.7 | all-reduce | flops 2 | bytes 16 | tf_op jit(solution)/shard_map/psum | solution.py:15
  275.5 9.6 %all-reduce.24 = (f32[]{:T(128)}, f32[]{:T(128)}) all-reduce(f32[]{:T(128)} %get-tuple-element.10, f32[]{:T(128)} %get-tuple-element.11), channel_id=1, replica_groups=mesh['tm_0'=4,'tm_1'=4,'env_0'=4,'env_1'=2] {'tm_1'}, use_global_device_ids=true, to_apply=%region_7.8 | all-reduce | flops 2 | bytes 16 | tf_op jit(solution)/shard_map/psum | solution.py:15
  285.1 10.8 %all-reduce.22 = (f32[]{:T(128)}, f32[]{:T(128)}) all-reduce(f32[]{:T(128)} %get-tuple-element.6, f32[]{:T(128)} %get-tuple-element.7), channel_id=1, replica_groups=mesh['tm_0'=4,'tm_1'=4,'env_0'=4,'env_1'=2] {'env_0'}, use_global_device_ids=true, to_apply=%region_8.9 | all-reduce | flops 2 | bytes 16 | tf_op jit(solution)/shard_map/psum | solution.py:15
  299.7 5.0 %subtract_divide_fusion.1 = f32[2048,512]{0,1:T(8,128)} fusion(f32[2048,512]{0,1:T(8,128)} %get-tuple-element.20, f32[]{:T(128)S(6)} %sqrt.6, f32[]{:T(128)S(6)} %div.24), kind=kLoop, calls=%fused_computation.39 | loop fusion | flops 2097152 | bytes 8388616 | tf_op jit(solution)/shard_map/div | solution.py:122
  304.6 8.4 %all-to-all-start.1 = ((f32[16,32,2048]{2,1,0:T(8,128)}), f32[16,32,2048]{2,1,0:T(8,128)}, u32[]{:S(2)}, u32[]{:S(2)}) async-start(f32[16,32,2048]{2,1,0:T(8,128)} %bitcast.24), calls=%async_computation.1 | async-start | bytes 8388608 | tf_op jit(solution)/shard_map/all_to_all | solution.py:149
  313.7 5.0 %subtract_divide_fusion = f32[2048,512]{0,1:T(8,128)} fusion(f32[2048,512]{0,1:T(8,128)} %get-tuple-element.19, f32[]{:T(128)S(6)} %sqrt.7, f32[]{:T(128)S(6)} %div.28), kind=kLoop, calls=%fused_computation.38 | loop fusion | flops 2097152 | bytes 8388616 | tf_op jit(solution)/shard_map/div | solution.py:123
  318.7 56.0 %all-to-all-done.1 = f32[16,32,2048]{2,1,0:T(8,128)} async-done(((f32[16,32,2048]{2,1,0:T(8,128)}), f32[16,32,2048]{2,1,0:T(8,128)}, u32[]{:S(2)}, u32[]{:S(2)}) %all-to-all-start.1) | async-done | bytes 4194336 | tf_op jit(solution)/shard_map/all_to_all | solution.py:149
  374.7 6.9 %all-to-all-start.2 = ((f32[16,32,2048]{2,1,0:T(8,128)}), f32[16,32,2048]{2,1,0:T(8,128)}, u32[]{:S(2)}, u32[]{:S(2)}) async-start(f32[16,32,2048]{2,1,0:T(8,128)} %bitcast.25), calls=%async_computation.2 | async-start | bytes 8388608 | tf_op jit(solution)/shard_map/all_to_all | solution.py:150
  381.7 4.7 %copy.37 = f32[16,4,8,2048]{3,2,0,1:T(8,128)} copy(f32[16,4,8,2048]{3,2,1,0:T(8,128)} %bitcast.16) | data formatting | bytes 8388608 | tf_op jit(solution)/shard_map/all_to_all | solution.py:149
  386.4 54.2 %all-to-all-done.2 = f32[16,32,2048]{2,1,0:T(8,128)} async-done(((f32[16,32,2048]{2,1,0:T(8,128)}), f32[16,32,2048]{2,1,0:T(8,128)}, u32[]{:S(2)}, u32[]{:S(2)}) %all-to-all-start.2) | async-done | bytes 4194336 | tf_op jit(solution)/shard_map/all_to_all | solution.py:150
  440.6 4.7 %copy.38 = f32[16,4,8,2048]{3,2,0,1:T(8,128)} copy(f32[16,4,8,2048]{3,2,1,0:T(8,128)} %bitcast.18) | data formatting | bytes 8388608 | tf_op jit(solution)/shard_map/all_to_all | solution.py:150
  (88 shorter events, 34.0 us)
Async XLA Ops:
  1.4 19.9 %collective-permute-start = (f32[1,512]{1,0:T(1,128)S(1)}, f32[1,512]{1,0:T(1,128)S(1)}, u32[]{:S(2)}, u32[]{:S(2)}) collective-permute-start(f32[1,512]{1,0:T(1,128)S(1)} %slice.161), channel_id=1, source_target_pairs={{8,0},{16,8},{24,16},{32,24},{40,32},{48,40},{56,48},{64,56},{72,6... | collective-permute-start | bytes 6152 | tf_op jit(solution)/shard_map/ppermute | solution.py:22
  15.9 5.4 %copy-start.19 = (f32[512]{0:T(512)S(1)}, f32[512]{0:T(512)}, u32[]{:S(2)}) copy-start(f32[512]{0:T(512)} %param.9) | copy-start | bytes 6148
  27.4 1.2 copy-start.18
  41.8 3.4 copy-start
  58.5 5.5 %copy-start.2 = (f32[2048,512]{0,1:T(8,128)S(1)}, f32[2048,512]{0,1:T(8,128)}, u32[]{:S(2)}) copy-start(f32[2048,512]{0,1:T(8,128)} %get-tuple-element.38) | copy-start | bytes 12582916
  64.0 3.1 copy-start.1
  77.3 5.5 %copy-start.4 = (f32[2048,512]{0,1:T(8,128)S(1)}, f32[2048,512]{0,1:T(8,128)}, u32[]{:S(2)}) copy-start(f32[2048,512]{0,1:T(8,128)} %get-tuple-element.36) | copy-start | bytes 12582916
  82.8 3.1 copy-start.3
  96.3 5.5 %copy-start.6 = (f32[2048,512]{0,1:T(8,128)S(1)}, f32[2048,512]{0,1:T(8,128)}, u32[]{:S(2)}) copy-start(f32[2048,512]{0,1:T(8,128)} %get-tuple-element.34) | copy-start | bytes 12582916
  101.8 3.1 copy-start.5
  115.0 5.5 %copy-start.8 = (f32[2048,512]{0,1:T(8,128)S(1)}, f32[2048,512]{0,1:T(8,128)}, u32[]{:S(2)}) copy-start(f32[2048,512]{0,1:T(8,128)} %get-tuple-element.32) | copy-start | bytes 12582916
  120.5 3.1 copy-start.7
  133.8 4.4 copy-start.9
  151.5 4.2 copy-start.10
  164.4 4.0 copy-start.11
  168.4 3.5 copy-start.12
  179.9 3.4 copy-start.13
  183.3 3.3 copy-start.14
  193.3 2.0 copy-start.17
  195.4 2.8 copy-start.15
  199.1 2.0 copy-start.16
  201.9 11.1 %all-to-all-start = ((f32[16,2,512]{2,1,0:T(2,128)}), f32[16,2,512]{2,1,0:T(2,128)S(1)}, u32[]{:S(2)}, u32[]{:S(2)}) async-start(f32[16,2,512]{2,1,0:T(2,128)} %broadcast_in_dim.20), calls=%async_computation | async-start | bytes 131072 | tf_op jit(solution)/shard_map/all_to_all | solution.py:27
  304.6 70.1 %all-to-all-start.1 = ((f32[16,32,2048]{2,1,0:T(8,128)}), f32[16,32,2048]{2,1,0:T(8,128)}, u32[]{:S(2)}, u32[]{:S(2)}) async-start(f32[16,32,2048]{2,1,0:T(8,128)} %bitcast.24), calls=%async_computation.1 | async-start | bytes 8388608 | tf_op jit(solution)/shard_map/all_to_all | solution.py:149
  374.7 65.8 %all-to-all-start.2 = ((f32[16,32,2048]{2,1,0:T(8,128)}), f32[16,32,2048]{2,1,0:T(8,128)}, u32[]{:S(2)}, u32[]{:S(2)}) async-start(f32[16,32,2048]{2,1,0:T(8,128)} %bitcast.25), calls=%async_computation.2 | async-start | bytes 8388608 | tf_op jit(solution)/shard_map/all_to_all | solution.py:150
where the time goes:
time: 453 us; the launch traced here: 445 us
  other arithmetic  133 us (29%)
  waiting for transfers between devices  114 us (25%)
  local copies, waits for them, and re-layouts  106 us (23%)
  blocking collectives  63.7 us (14%)
  starting transfers between devices  24.8 us (5%)
    add x10, other arithmetic, suffix_scan(): partial_value = partial_value + decayed * later_partial  89.9 us
    slice x22, local copies, waits for them, and re-layouts, shift_later(): kept = lax.slice_in_dim(field, distance, length, 1, axis)  69.8 us
    psum x8, blocking collectives, by_axis(): value = lax.psum(value, axis)  63.7 us
    all_to_all x1, waiting for transfers between devices, shards(): lax.all_to_all(norm_adv.T, TM, split_axis=0, concat_axis=1, tiled=True)  56 us
    all_to_all x1, waiting for transfers between devices, shards(): lax.all_to_all(norm_ret.T, TM, split_axis=0, concat_axis=1, tiled=True)  54.2 us
    unnamed x42, local copies, waits for them, and re-layouts  18.3 us
    reduce_sum x1, other arithmetic, statistics(): jnp.sum(returns)  11.1 us
  transfers between devices with their start and end apart: 4, of which 3 were waited for; matrix products, arithmetic and copies ran while one was open for 6% of the time, Pallas kernels for 0%

commit v1 on v0

--- a/solution.py
+++ b/solution.py
@@ -12,7 +12,7 @@
 
 def by_axis(value, axes):
     for axis in axes:
-        value = lax.psum(value, axis)
+        value = jnp.sum(lax.all_gather(value, axis), axis=0)
     return value
 
 

time: 453 us -> 481 us (1.062)
  local copies, waits for them, and re-layouts: 106 us -> 129 us
  other arithmetic: 133 us -> 143 us
  blocking collectives: 63.7 us -> 58.1 us
    psum x8 -> x0, blocking collectives: 63.7 us -> none  [by_axis(): value = lax.psum(value, axis)]
    unnamed x0 -> x8, blocking collectives: none -> 58.1 us
    unnamed x42 -> x78, local copies, waits for them, and re-layouts: 18.3 us -> 41.5 us
    reduce_sum x0 -> x16, other arithmetic: none -> 10.5 us  [by_axis(): value = jnp.sum(lax.all_gather(value, axis), axis=0)]
where the time goes in v1:
time: 481 us; the launch traced here: 473 us
  other arithmetic  143 us (30%)
  local copies, waits for them, and re-layouts  129 us (27%)
  waiting for transfers between devices  114 us (24%)
  blocking collectives  58.1 us (12%)
  starting transfers between devices  24.7 us (5%)
    add x10, other arithmetic, suffix_scan(): partial_value = partial_value + decayed * later_partial  90 us
    slice x22, local copies, waits for them, and re-layouts, shift_later(): kept = lax.slice_in_dim(field, distance, length, 1, axis)  68.8 us
    unnamed x8, blocking collectives  58.1 us
    all_to_all x1, waiting for transfers between devices, shards(): lax.all_to_all(norm_ret.T, TM, split_axis=0, concat_axis=1, tiled=True)  55.4 us
    all_to_all x1, waiting for transfers between devices, shards(): lax.all_to_all(norm_adv.T, TM, split_axis=0, concat_axis=1, tiled=True)  54.2 us
    unnamed x78, local copies, waits for them, and re-layouts  41.5 us
    reduce_sum x1, other arithmetic, statistics(): jnp.sum(returns)  11.1 us
    reduce_sum x16, other arithmetic, by_axis(): value = jnp.sum(lax.all_gather(value, axis), axis=0)  10.5 us
  transfers between devices with their start and end apart: 4, of which 3 were waited for; matrix products, arithmetic and copies ran while one was open for 6% of the time, Pallas kernels for 0%

profile of v1, /device:TPU:114, one launch (start us, length us, event | category | flops | bytes accessed | tf_op | source)
XLA Modules:
  0.0 472.8 jit_solution(8164486393100877218)
XLA Ops:
  5.2 5.3 %copy.25 = f32[2048,512]{0,1:T(8,128)} copy(f32[2048,512]{1,0:T(8,128)} %param.8) | data formatting | bytes 8388608 | tf_op args[1]
  10.6 5.3 %slice.207 = f32[2047,512]{0,1:T(8,128)} slice(f32[2048,512]{0,1:T(8,128)} %copy.25), slice={[1:2048], [0:512]} | slice | bytes 8384512 | tf_op jit(solution)/shard_map/slice | solution.py:139
  15.9 5.4 %copy.27 = f32[2048,512]{0,1:T(8,128)} copy(f32[2048,512]{1,0:T(8,128)} %param.7) | data formatting | bytes 8388608 | tf_op args[0]
  22.0 6.0 %fusion.3 = f32[2048,512]{0,1:T(8,128)S(1)} fusion(f32[2048,512]{0,1:T(8,128)} %copy.25, f32[2048,512]{0,1:T(8,128)} %copy.27, f32[1,512]{0,1:T(8,128)S(1)} %copy.26, f32[2047,512]{0,1:T(8,128)} %slice.207, f32[512]{0:T(512)S(1)} %get-tuple-element.54, s32[512]{0:T(512)S(1)} %bitcast.54, s32[512]{0:T(512)S(1)} %bitcast.57, s32[512]{0:T(512)S(1)} %bitcast.51, ...), kind=kLoop, calls=%fused_computation.9 | loop fusion | flops 14680064 | bytes 16795648 | tf_op jit(solution)/shard_map/sub | solution.py:140
  29.2 5.3 %multiply_multiply_fusion = (f32[2048,512]{0,1:T(8,128)S(1)}, f32[2048,512]{0,1:T(8,128)S(1)}) fusion(s32[512]{0:T(512)S(1)} %copy-done.14, f32[512]{0:T(512)S(1)} %get-tuple-element.53, s32[2048]{0:T(1024)S(1)} %iota_add_fusion, s32[512]{0:T(512)S(1)} %bitcast.55, s32[512]{0:T(512)S(1)} %bitcast.58, s32[512]{0:T(512)S(1)} %bitcast.52, s32[512]{0:T(512)S(1)} %bitcast.49, ...), kind=kLoop, calls=%fused_computation.35 | loop fusion | flops 29360128 | bytes 16795648 | tf_op jit(solution)/shard_map/mul | solution.py:141
  36.7 5.7 %multiply_add_fusion.10 = (f32[2048,512]{0,1:T(8,128)S(1)}, f32[2048,512]{0,1:T(8,128)S(1)}) fusion(f32[2048,512]{0,1:T(8,128)S(1)} %get-tuple-element.44, f32[2046,512]{0,1:T(8,128)S(1)} %slice.210, f32[2047,512]{0,1:T(8,128)S(1)} %slice.209, s32[512]{0:T(512)S(1)} %copy-done.14, s32[512]{0:T(512)S(1)} %bitcast.56, s32[512]{0:T(512)S(1)} %bitcast.59, ...), kind=kLoop, calls=%fused_computation.32 | loop fusion | flops 30408704 | bytes 20985856 | tf_op jit(solution)/shard_map/add | solution.py:98
  42.5 3.2 slice.211
  45.7 3.2 slice.212
  48.8 10.2 %multiply_add_fusion.9 = (f32[2048,512]{0,1:T(8,128)}, f32[2048,512]{0,1:T(8,128)}) fusion(f32[2048,512]{0,1:T(8,128)S(1)} %get-tuple-element.39, f32[2044,512]{0,1:T(8,128)} %slice.212, f32[2048,512]{0,1:T(8,128)} %copy-done, f32[2046,512]{0,1:T(8,128)} %slice.211), kind=kLoop, calls=%fused_computation.30 | loop fusion | flops 3145728 | bytes 25153536 | tf_op jit(solution)/shard_map/add | solution.py:98
  59.0 5.5 %slice.213 = f32[2044,512]{0,1:T(8,128)} slice(f32[2048,512]{0,1:T(8,128)} %get-tuple-element.38), slice={[4:2048], [0:512]} | slice | bytes 8372224 | tf_op jit(solution)/shard_map/slice | solution.py:83
  64.5 3.2 slice.214
  67.6 10.2 %multiply_add_fusion.8 = (f32[2048,512]{0,1:T(8,128)}, f32[2048,512]{0,1:T(8,128)}) fusion(f32[2048,512]{0,1:T(8,128)S(1)} %copy-done.1, f32[2040,512]{0,1:T(8,128)} %slice.214, f32[2048,512]{0,1:T(8,128)} %get-tuple-element.38, f32[2044,512]{0,1:T(8,128)} %slice.213), kind=kLoop, calls=%fused_computation.28 | loop fusion | flops 3145728 | bytes 25141248 | tf_op jit(solution)/shard_map/add | solution.py:98
  77.8 5.5 %slice.215 = f32[2040,512]{0,1:T(8,128)} slice(f32[2048,512]{0,1:T(8,128)} %get-tuple-element.36), slice={[8:2048], [0:512]} | slice | bytes 8355840 | tf_op jit(solution)/shard_map/slice | solution.py:83
  83.3 3.2 slice.216
  86.5 10.6 %multiply_add_fusion.7 = (f32[2048,512]{0,1:T(8,128)}, f32[2048,512]{0,1:T(8,128)}) fusion(f32[2048,512]{0,1:T(8,128)S(1)} %copy-done.2, f32[2032,512]{0,1:T(8,128)} %slice.216, f32[2048,512]{0,1:T(8,128)} %get-tuple-element.36, f32[2040,512]{0,1:T(8,128)} %slice.215), kind=kLoop, calls=%fused_computation.26 | loop fusion | flops 3145728 | bytes 25116672 | tf_op jit(solution)/shard_map/add | solution.py:98
  97.0 5.5 %slice.217 = f32[2032,512]{0,1:T(8,128)} slice(f32[2048,512]{0,1:T(8,128)} %get-tuple-element.34), slice={[16:2048], [0:512]} | slice | bytes 8323072 | tf_op jit(solution)/shard_map/slice | solution.py:83
  102.5 3.2 slice.218
  105.7 10.2 %multiply_add_fusion.6 = (f32[2048,512]{0,1:T(8,128)}, f32[2048,512]{0,1:T(8,128)}) fusion(f32[2048,512]{0,1:T(8,128)S(1)} %copy-done.3, f32[2016,512]{0,1:T(8,128)} %slice.218, f32[2048,512]{0,1:T(8,128)} %get-tuple-element.34, f32[2032,512]{0,1:T(8,128)} %slice.217), kind=kLoop, calls=%fused_computation.24 | loop fusion | flops 3145728 | bytes 25067520 | tf_op jit(solution)/shard_map/add | solution.py:98
  115.9 5.5 %slice.219 = f32[2016,512]{0,1:T(8,128)} slice(f32[2048,512]{0,1:T(8,128)} %get-tuple-element.32), slice={[32:2048], [0:512]} | slice | bytes 8257536 | tf_op jit(solution)/shard_map/slice | solution.py:83
  121.3 3.2 slice.220
  124.5 10.2 %multiply_add_fusion.5 = (f32[2048,512]{0,1:T(8,128)}, f32[2048,512]{0,1:T(8,128)}) fusion(f32[2048,512]{0,1:T(8,128)S(1)} %copy-done.4, f32[1984,512]{0,1:T(8,128)} %slice.220, f32[2048,512]{0,1:T(8,128)} %get-tuple-element.32, f32[2016,512]{0,1:T(8,128)} %slice.219), kind=kLoop, calls=%fused_computation.22 | loop fusion | flops 3145728 | bytes 24969216 | tf_op jit(solution)/shard_map/add | solution.py:98
  134.7 5.5 %slice.221 = f32[1984,512]{0,1:T(8,128)} slice(f32[2048,512]{0,1:T(8,128)} %get-tuple-element.30), slice={[64:2048], [0:512]} | slice | bytes 8126464 | tf_op jit(solution)/shard_map/slice | solution.py:83
  143.8 9.9 %multiply_add_fusion.4 = (f32[2048,512]{0,1:T(8,128)}, f32[2048,512]{0,1:T(8,128)}) fusion(f32[2048,512]{0,1:T(8,128)} %get-tuple-element.29, f32[1920,512]{0,1:T(8,128)} %slice.222, f32[2048,512]{0,1:T(8,128)S(1)} %copy-done.5, f32[1984,512]{0,1:T(8,128)} %slice.221), kind=kLoop, calls=%fused_computation.20 | loop fusion | flops 3145728 | bytes 24772608 | tf_op jit(solution)/shard_map/add | solution.py:98
  153.7 2.5 slice.223
  159.1 8.3 %multiply_add_fusion.3 = (f32[2048,512]{0,1:T(8,128)}, f32[2048,512]{0,1:T(8,128)}) fusion(f32[2048,512]{0,1:T(8,128)} %get-tuple-element.27, f32[1792,512]{0,1:T(8,128)} %slice.224, f32[2048,512]{0,1:T(8,128)S(1)} %copy-done.7, f32[1920,512]{0,1:T(8,128)S(1)} %slice.223), kind=kLoop, calls=%fused_computation.18 | loop fusion | flops 3145728 | bytes 24379392 | tf_op jit(solution)/shard_map/add | solution.py:98
  167.4 4.2 slice.225
  175.0 8.0 %multiply_add_fusion.2 = (f32[2048,512]{0,1:T(8,128)}, f32[2048,512]{0,1:T(8,128)}) fusion(f32[2048,512]{0,1:T(8,128)S(1)} %copy-done.10, f32[1536,512]{0,1:T(8,128)} %slice.226, f32[2048,512]{0,1:T(8,128)S(1)} %copy-done.9, f32[1792,512]{0,1:T(8,128)} %slice.225), kind=kLoop, calls=%fused_computation.16 | loop fusion | flops 3145728 | bytes 23592960 | tf_op jit(solution)/shard_map/add | solution.py:98
  183.0 3.9 slice.227
  189.3 6.7 %multiply_add_fusion.1 = (f32[2048,512]{0,1:T(8,128)}, f32[2048,512]{0,1:T(8,128)S(1)}) fusion(f32[2048,512]{0,1:T(8,128)S(1)} %copy-done.12, f32[1024,512]{0,1:T(8,128)} %slice.228, f32[2048,512]{0,1:T(8,128)S(1)} %copy-done.11, f32[1536,512]{0,1:T(8,128)} %slice.227), kind=kLoop, calls=%fused_computation.14 | loop fusion | flops 3145728 | bytes 22020096 | tf_op jit(solution)/shard_map/add | solution.py:98
  200.8 7.1 %all-to-all-start = ((f32[16,2,512]{2,1,0:T(2,128)}), f32[16,2,512]{2,1,0:T(2,128)S(1)}, u32[]{:S(2)}, u32[]{:S(2)}) async-start(f32[16,2,512]{2,1,0:T(2,128)} %broadcast_in_dim.20), calls=%async_computation | async-start | bytes 131072 | tf_op jit(solution)/shard_map/all_to_all | solution.py:27
  207.9 4.0 all-to-all-done
  212.7 11.1 %fusion.6 = (f32[]{:T(128)}, f32[2048,512]{0,1:T(8,128)}, f32[2048,512]{0,1:T(8,128)}) fusion(f32[2048,512]{0,1:T(8,128)} %copy.25, f32[2048,512]{0,1:T(8,128)} %get-tuple-element.21, f32[2048,512]{0,1:T(8,128)} %copy-done.13, f32[512]{0:T(512)S(1)} %bitcast.60), kind=kLoop, calls=%fused_computation.55 | loop fusion | flops 4194303 | bytes 20973572 | tf_op jit(solution)/shard_map/reduce_sum | solution.py:111
  223.8 4.0 reduce_sum.180
  231.1 8.5 %all-reduce.43 = (f32[4]{0:T(128)S(1)}, f32[4]{0:T(128)S(1)}) all-reduce(f32[4]{0:T(128)S(1)} %dynamic-update-slice, f32[4]{0:T(128)S(1)} %dynamic-update-slice.8), channel_id=1, replica_groups=mesh['tm_0'=4,'tm_1'=4,'env_0'=4,'env_1'=2] {'tm_0'}, use_global_device_ids=true, to_apply=%add.22 | all-reduce | flops 8 | bytes 64
  244.2 8.5 %all-reduce.41 = (f32[4]{0:T(128)S(1)}, f32[4]{0:T(128)S(1)}) all-reduce(f32[4]{0:T(128)S(1)} %dynamic-update-slice.1, f32[4]{0:T(128)S(1)} %dynamic-update-slice.9), channel_id=1, replica_groups=mesh['tm_0'=4,'tm_1'=4,'env_0'=4,'env_1'=2] {'tm_1'}, use_global_device_ids=true, to_apply=%add.23 | all-reduce | flops 8 | bytes 64
  257.2 8.6 %all-reduce.39 = (f32[4]{0:T(128)S(1)}, f32[4]{0:T(128)S(1)}) all-reduce(f32[4]{0:T(128)S(1)} %dynamic-update-slice.2, f32[4]{0:T(128)S(1)} %dynamic-update-slice.10), channel_id=1, replica_groups=mesh['tm_0'=4,'tm_1'=4,'env_0'=4,'env_1'=2] {'env_0'}, use_global_device_ids=true, to_apply=%add.24 | all-reduce | flops 8 | bytes 64
  275.1 5.2 %multiply_reduce_fusion = (f32[]{:T(128)}, f32[]{:T(128)}) fusion(f32[2048,512]{0,1:T(8,128)} %get-tuple-element.19, f32[]{:T(128)S(6)} %div.28, f32[2048,512]{0,1:T(8,128)} %get-tuple-element.20, f32[]{:T(128)S(6)} %div.24), kind=kLoop, calls=%fused_computation.10 | loop fusion | flops 6291454 | bytes 8388624 | tf_op jit(solution)/shard_map/reduce_sum | solution.py:118
  283.0 8.6 %all-reduce.42 = (f32[4]{0:T(128)S(1)}, f32[4]{0:T(128)S(1)}) all-reduce(f32[4]{0:T(128)S(1)} %dynamic-update-slice.4, f32[4]{0:T(128)S(1)} %dynamic-update-slice.12), channel_id=1, replica_groups=mesh['tm_0'=4,'tm_1'=4,'env_0'=4,'env_1'=2] {'tm_0'}, use_global_device_ids=true, to_apply=%add.26 | all-reduce | flops 8 | bytes 64
  295.8 9.0 %all-reduce.40 = (f32[4]{0:T(128)S(1)}, f32[4]{0:T(128)S(1)}) all-reduce(f32[4]{0:T(128)S(1)} %dynamic-update-slice.5, f32[4]{0:T(128)S(1)} %dynamic-update-slice.13), channel_id=1, replica_groups=mesh['tm_0'=4,'tm_1'=4,'env_0'=4,'env_1'=2] {'tm_1'}, use_global_device_ids=true, to_apply=%add.27 | all-reduce | flops 8 | bytes 64
  308.8 10.1 %all-reduce.38 = (f32[4]{0:T(128)S(1)}, f32[4]{0:T(128)S(1)}) all-reduce(f32[4]{0:T(128)S(1)} %dynamic-update-slice.6, f32[4]{0:T(128)S(1)} %dynamic-update-slice.14), channel_id=1, replica_groups=mesh['tm_0'=4,'tm_1'=4,'env_0'=4,'env_1'=2] {'env_0'}, use_global_device_ids=true, to_apply=%add.28 | all-reduce | flops 8 | bytes 64
  327.0 5.0 %subtract_divide_fusion = f32[2048,512]{0,1:T(8,128)} fusion(f32[2048,512]{0,1:T(8,128)} %get-tuple-element.19, f32[]{:T(128)S(6)} %sqrt.7, f32[]{:T(128)S(6)} %div.28), kind=kLoop, calls=%fused_computation.38 | loop fusion | flops 2097152 | bytes 8388616 | tf_op jit(solution)/shard_map/div | solution.py:123
  332.0 8.4 %all-to-all-start.2 = ((f32[16,32,2048]{2,1,0:T(8,128)}), f32[16,32,2048]{2,1,0:T(8,128)}, u32[]{:S(2)}, u32[]{:S(2)}) async-start(f32[16,32,2048]{2,1,0:T(8,128)} %bitcast.44), calls=%async_computation.2 | async-start | bytes 8388608 | tf_op jit(solution)/shard_map/all_to_all | solution.py:150
  341.7 5.0 %subtract_divide_fusion.1 = f32[2048,512]{0,1:T(8,128)} fusion(f32[2048,512]{0,1:T(8,128)} %get-tuple-element.20, f32[]{:T(128)S(6)} %sqrt.6, f32[]{:T(128)S(6)} %div.24), kind=kLoop, calls=%fused_computation.39 | loop fusion | flops 2097152 | bytes 8388616 | tf_op jit(solution)/shard_map/div | solution.py:122
  346.7 55.4 %all-to-all-done.2 = f32[16,32,2048]{2,1,0:T(8,128)} async-done(((f32[16,32,2048]{2,1,0:T(8,128)}), f32[16,32,2048]{2,1,0:T(8,128)}, u32[]{:S(2)}, u32[]{:S(2)}) %all-to-all-start.2) | async-done | bytes 4194336 | tf_op jit(solution)/shard_map/all_to_all | solution.py:150
  402.1 6.9 %all-to-all-start.1 = ((f32[16,32,2048]{2,1,0:T(8,128)}), f32[16,32,2048]{2,1,0:T(8,128)}, u32[]{:S(2)}, u32[]{:S(2)}) async-start(f32[16,32,2048]{2,1,0:T(8,128)} %bitcast.45), calls=%async_computation.1 | async-start | bytes 8388608 | tf_op jit(solution)/shard_map/all_to_all | solution.py:149
  409.0 4.7 copy.38
  413.7 54.2 %all-to-all-done.1 = f32[16,32,2048]{2,1,0:T(8,128)} async-done(((f32[16,32,2048]{2,1,0:T(8,128)}), f32[16,32,2048]{2,1,0:T(8,128)}, u32[]{:S(2)}, u32[]{:S(2)}) %all-to-all-start.1) | async-done | bytes 4194336 | tf_op jit(solution)/shard_map/all_to_all | solution.py:149
  467.9 4.7 copy.37
  (140 shorter events, 66.0 us)
Async XLA Ops:
  1.4 20.5 %collective-permute-start = (f32[1,512]{1,0:T(1,128)S(1)}, f32[1,512]{1,0:T(1,128)S(1)}, u32[]{:S(2)}, u32[]{:S(2)}) collective-permute-start(f32[1,512]{1,0:T(1,128)S(1)} %slice.161), channel_id=1, source_target_pairs={{8,0},{16,8},{24,16},{32,24},{40,32},{48,40},{56,48},{64,56},{72,6... | collective-permute-start | bytes 6152 | tf_op jit(solution)/shard_map/ppermute | solution.py:22
  15.8 5.4 %copy-start.19 = (u32[128]{0:T(128)S(1)}, u32[128]{0:T(128)}, u32[]{:S(2)}) copy-start(u32[128]{0:T(128)} %constant.114) | copy-start | bytes 1540
  15.9 6.0 %copy-start.15 = (f32[512]{0:T(512)S(1)}, f32[512]{0:T(512)}, u32[]{:S(2)}) copy-start(f32[512]{0:T(512)} %param.9) | copy-start | bytes 6148
  28.0 1.2 copy-start.14
  42.4 3.2 copy-start
  59.0 5.5 %copy-start.1 = (f32[2048,512]{0,1:T(8,128)S(1)}, f32[2048,512]{0,1:T(8,128)}, u32[]{:S(2)}) copy-start(f32[2048,512]{0,1:T(8,128)} %get-tuple-element.37) | copy-start | bytes 12582916
  77.8 5.5 %copy-start.2 = (f32[2048,512]{0,1:T(8,128)S(1)}, f32[2048,512]{0,1:T(8,128)}, u32[]{:S(2)}) copy-start(f32[2048,512]{0,1:T(8,128)} %get-tuple-element.35) | copy-start | bytes 12582916
  97.0 5.5 %copy-start.3 = (f32[2048,512]{0,1:T(8,128)S(1)}, f32[2048,512]{0,1:T(8,128)}, u32[]{:S(2)}) copy-start(f32[2048,512]{0,1:T(8,128)} %get-tuple-element.33) | copy-start | bytes 12582916
  115.9 5.5 %copy-start.4 = (f32[2048,512]{0,1:T(8,128)S(1)}, f32[2048,512]{0,1:T(8,128)}, u32[]{:S(2)}) copy-start(f32[2048,512]{0,1:T(8,128)} %get-tuple-element.31) | copy-start | bytes 12582916
  134.7 5.5 %copy-start.6 = (f32[2048,512]{0,1:T(8,128)S(1)}, f32[2048,512]{0,1:T(8,128)}, u32[]{:S(2)}) copy-start(f32[2048,512]{0,1:T(8,128)} %get-tuple-element.29) | copy-start | bytes 12582916
  140.2 3.6 copy-start.5
  153.7 3.4 copy-start.8
  156.2 2.9 copy-start.7
  167.4 4.3 copy-start.10
  171.7 3.3 copy-start.9
  183.0 3.9 copy-start.12
  183.0 6.3 %copy-start.11 = (f32[2048,512]{0,1:T(8,128)S(1)}, f32[2048,512]{0,1:T(8,128)}, u32[]{:S(2)}) copy-start(f32[2048,512]{0,1:T(8,128)} %get-tuple-element.24) | copy-start | bytes 12582916
  196.9 1.9 copy-start.13
  200.8 11.1 %all-to-all-start = ((f32[16,2,512]{2,1,0:T(2,128)}), f32[16,2,512]{2,1,0:T(2,128)S(1)}, u32[]{:S(2)}, u32[]{:S(2)}) async-start(f32[16,2,512]{2,1,0:T(2,128)} %broadcast_in_dim.20), calls=%async_computation | async-start | bytes 131072 | tf_op jit(solution)/shard_map/all_to_all | solution.py:27
  223.7 6.7 %copy-start.18 = (u32[128]{0:T(128)S(1)}, u32[128]{0:T(128)}, u32[]{:S(2)}) copy-start(u32[128]{0:T(128)} %constant.119) | copy-start | bytes 1540
  223.7 19.9 %copy-start.17 = (u32[128]{0:T(128)S(1)}, u32[128]{0:T(128)}, u32[]{:S(2)}) copy-start(u32[128]{0:T(128)} %constant.124) | copy-start | bytes 1540
  223.7 32.9 %copy-start.16 = (u32[128]{0:T(128)S(1)}, u32[128]{0:T(128)}, u32[]{:S(2)}) copy-start(u32[128]{0:T(128)} %constant.129) | copy-start | bytes 1540
  332.0 70.1 %all-to-all-start.2 = ((f32[16,32,2048]{2,1,0:T(8,128)}), f32[16,32,2048]{2,1,0:T(8,128)}, u32[]{:S(2)}, u32[]{:S(2)}) async-start(f32[16,32,2048]{2,1,0:T(8,128)} %bitcast.44), calls=%async_computation.2 | async-start | bytes 8388608 | tf_op jit(solution)/shard_map/all_to_all | solution.py:150
  402.1 65.8 %all-to-all-start.1 = ((f32[16,32,2048]{2,1,0:T(8,128)}), f32[16,32,2048]{2,1,0:T(8,128)}, u32[]{:S(2)}, u32[]{:S(2)}) async-start(f32[16,32,2048]{2,1,0:T(8,128)} %bitcast.45), calls=%async_computation.1 | async-start | bytes 8388608 | tf_op jit(solution)/shard_map/all_to_all | solution.py:149
